TPU v7x, 256 devices: a whole 4x4x8 slice. The times are simulated.
256 devices in a mesh: chan: 32 (over z, x_lo, core), day: 8 (over x_hi, y).
Axes of the slice: x: 4 (x_hi: 2, x_lo: 2; x = x_hi * 2 + x_lo), y: 4, z: 8, core: 2. Of those that a mesh axis runs over, the one named last changes fastest.
Arguments:
- spectra: bfloat16 [8, 512, 2, 4096], P('day', 'chan'), may hold values from -6 to 6
- source_index: int32 [16], replicated, may hold values from 0 to 511, as said below
- interrogator: int32 [512], P('chan'), may hold values from 0 to 7, as said below
- lag_bounds: int32 [16, 2], replicated, may hold values from 0 to 256, as said below
Outputs:
- reference_stack: bfloat16 [16, 512, 256], P('day', 'chan')
- drift: float32 [8, 8], P('day')
Inputs may be any that keep to these rules, and one draw needn't show every extreme that they name: `source_index`: distinct channels. Each interrogator serves one contiguous run of channels, in rising order, of at least 32 channels. `lag_bounds`: first lag below end lag, and each window spans at least 128 lags.
All inputs are finite; a program needn't handle non-finite values.
Results may differ from a plain program's by a relative error of at most 0.0065.
Values may be sent and summed in bfloat16 or wider, within the bound.
No kernel may reach another device: no remote copies, remote signals or barrier semaphores. Data moves between devices by JAX's collectives and lax.ppermute only.
A program may use at most 64 MiB of HBM per device.

v0:
```python
import math
import jax
import jax.numpy as jnp
from jax import lax
from jax.sharding import PartitionSpec as P

LAGS = 256
NINT = 8


def from_root(value, axis, source):
    kept = jnp.where(lax.axis_index(axis) == source, value, 0).astype(value.dtype)
    return lax.psum(kept, axis)


def lag_table(bins, lags):
    freq = jnp.arange(bins, dtype=jnp.int32)
    shift = jnp.arange(lags, dtype=jnp.int32) - lags // 2
    phase = freq[:, None] * shift[None, :] % (2 * bins)
    angle = math.pi * phase.astype(jnp.float32) / bins
    scale = 1.0 / math.sqrt(bins)
    return jnp.concatenate([jnp.cos(angle) * scale, -jnp.sin(angle) * scale], 0).astype(
        jnp.bfloat16
    )


def per_device(spectra, source_index, interrogator, lag_bounds):
    day_dev, ch_dev, _, bins = spectra.shape
    nsrc = source_index.shape[0]
    lags = LAGS

    def fetch(source, buffer):
        chosen_chan = source_index[source]
        owner = chosen_chan // ch_dev
        local_row = chosen_chan - owner * ch_dev
        piece = lax.dynamic_slice_in_dim(spectra, local_row, 1, 1)
        arrived = from_root(piece, "chan", owner)
        return lax.dynamic_update_slice_in_dim(buffer, arrived, source, 1)

    sources = lax.fori_loop(0, nsrc, fetch, jnp.zeros((day_dev, nsrc, 2, bins), jnp.bfloat16))
    table = lag_table(bins, lags)
    block = math.gcd(nsrc, 16)

    def correlate_block(index, corr):
        chosen = sources[0].astype(jnp.float32)
        local = spectra[0].astype(jnp.float32)
        real_in = local[None, :, 0]
        imag_in = local[None, :, 1]
        real_src = chosen[:, None, 0]
        imag_src = chosen[:, None, 1]
        cross = jnp.concatenate(
            [real_in * real_src + imag_in * imag_src, imag_in * real_src - real_in * imag_src], -1
        )
        cross = cross.astype(jnp.bfloat16).reshape(block * ch_dev, 2 * bins)
        result = jnp.dot(cross, table, preferred_element_type=jnp.float32).reshape(
            1, block, ch_dev, lags
        )
        return result

    corr = lax.fori_loop(
        0, nsrc // block, correlate_block, jnp.zeros((day_dev, nsrc, ch_dev, lags), jnp.float32)
    )
    local_sum = jnp.sum(corr, 0)
    days = day_dev * lax.axis_size("day")
    total = lax.psum(local_sum, "day")
    ref_full = (total / days).astype(jnp.bfloat16)
    share = nsrc // lax.axis_size("day")
    ref_out = lax.dynamic_slice_in_dim(ref_full, lax.axis_index("day") * share, share, 0)
    ref_float = ref_full.astype(jnp.float32)
    lag_pos = jnp.arange(lags, dtype=jnp.int32)
    window = (
        (lag_pos[None, :] >= lag_bounds[:, 0:1]) & (lag_pos[None, :] < lag_bounds[:, 1:2])
    ).astype(jnp.float32)
    member = (interrogator[:, None] == jnp.arange(NINT, dtype=jnp.int32)[None, :]).astype(
        jnp.float32
    )
    day_corr = corr[0]
    padded = jnp.pad(day_corr, ((0, 0), (0, 0), (1, 1)))
    slope = 0.5 * (padded[:, :, 2:] - padded[:, :, :-2])
    weighted = window[:, None, :] * slope
    num_chan = jnp.sum(weighted * (day_corr - ref_float), axis=(0, 2))
    den_chan = jnp.sum(weighted * slope, axis=(0, 2))
    numers = [jnp.sum(num_chan[:, None] * member, 0)]
    denoms = [jnp.sum(den_chan[:, None] * member, 0)]
    numer, denom = lax.psum((jnp.stack(numers, 0), jnp.stack(denoms, 0)), "chan")
    drift = numer / (denom + 1e-06)
    return (ref_out, drift)


def solution(mesh):
    return jax.shard_map(
        per_device,
        mesh=mesh,
        in_specs=(P("day", "chan", None, None), P(), P("chan"), P()),
        out_specs=(P("day", "chan", None), P("day", None)),
        check_vma=False,
    )
```

profile of v0, /device:TPU:1, one launch (start us, length us, event | category | flops | bytes accessed | tf_op | source)
XLA Modules:
  0.0 1944.4 jit_solution(5148934047910936278)
XLA Ops:
  9.0 1759.0 %while.19 = (s32[]{:T(128)}, bf16[1,16,2,4096]{3,2,1,0:T(2,128)(2,1)S(1)}, s32[16]{0:T(128)}, bf16[1,16,2,4096]{3,2,1,0:T(2,128)(2,1)}, s32[]{:T(128)}, /*index=...) while((s32[]{:T(128)}, ...), condition=%wide.region_2.3_spmd, body=%wide.region_0.2_spmd.sunk | while | flops 16410 | bytes 98691 | solution.py:40
  9.0 1.2 dynamic_slice.29
  14.2 107.7 %psum.39 = bf16[1,1,2,4096]{3,2,1,0:T(2,128)(2,1)S(1)} all-reduce(bf16[1,1,2,4096]{3,2,1,0:T(2,128)(2,1)S(1)} %broadcast_select_fusion.2), channel_id=1, replica_groups=mesh['chan'=32,'day'=8] {'chan'}, use_global_device_ids=true, to_apply=%region_1.1 | all-reduce | flops 8192 | bytes 32768 | tf_op jit(solution)/shard_map/while/body/eval_jaxpr/psum | solution.py:13
  127.2 104.5 %psum.39 = bf16[1,1,2,4096]{3,2,1,0:T(2,128)(2,1)S(1)} all-reduce(bf16[1,1,2,4096]{3,2,1,0:T(2,128)(2,1)S(1)} %broadcast_select_fusion.2), channel_id=1, replica_groups=mesh['chan'=32,'day'=8] {'chan'}, use_global_device_ids=true, to_apply=%region_1.1 | all-reduce | flops 8192 | bytes 32768 | tf_op jit(solution)/shard_map/while/body/eval_jaxpr/psum | solution.py:13
  236.9 104.5 %psum.39 = bf16[1,1,2,4096]{3,2,1,0:T(2,128)(2,1)S(1)} all-reduce(bf16[1,1,2,4096]{3,2,1,0:T(2,128)(2,1)S(1)} %broadcast_select_fusion.2), channel_id=1, replica_groups=mesh['chan'=32,'day'=8] {'chan'}, use_global_device_ids=true, to_apply=%region_1.1 | all-reduce | flops 8192 | bytes 32768 | tf_op jit(solution)/shard_map/while/body/eval_jaxpr/psum | solution.py:13
  346.7 104.5 %psum.39 = bf16[1,1,2,4096]{3,2,1,0:T(2,128)(2,1)S(1)} all-reduce(bf16[1,1,2,4096]{3,2,1,0:T(2,128)(2,1)S(1)} %broadcast_select_fusion.2), channel_id=1, replica_groups=mesh['chan'=32,'day'=8] {'chan'}, use_global_device_ids=true, to_apply=%region_1.1 | all-reduce | flops 8192 | bytes 32768 | tf_op jit(solution)/shard_map/while/body/eval_jaxpr/psum | solution.py:13
  451.1 1.2 dynamic_slice.29
  456.4 104.5 %psum.39 = bf16[1,1,2,4096]{3,2,1,0:T(2,128)(2,1)S(1)} all-reduce(bf16[1,1,2,4096]{3,2,1,0:T(2,128)(2,1)S(1)} %broadcast_select_fusion.2), channel_id=1, replica_groups=mesh['chan'=32,'day'=8] {'chan'}, use_global_device_ids=true, to_apply=%region_1.1 | all-reduce | flops 8192 | bytes 32768 | tf_op jit(solution)/shard_map/while/body/eval_jaxpr/psum | solution.py:13
  566.1 104.5 %psum.39 = bf16[1,1,2,4096]{3,2,1,0:T(2,128)(2,1)S(1)} all-reduce(bf16[1,1,2,4096]{3,2,1,0:T(2,128)(2,1)S(1)} %broadcast_select_fusion.2), channel_id=1, replica_groups=mesh['chan'=32,'day'=8] {'chan'}, use_global_device_ids=true, to_apply=%region_1.1 | all-reduce | flops 8192 | bytes 32768 | tf_op jit(solution)/shard_map/while/body/eval_jaxpr/psum | solution.py:13
  675.9 104.5 %psum.39 = bf16[1,1,2,4096]{3,2,1,0:T(2,128)(2,1)S(1)} all-reduce(bf16[1,1,2,4096]{3,2,1,0:T(2,128)(2,1)S(1)} %broadcast_select_fusion.2), channel_id=1, replica_groups=mesh['chan'=32,'day'=8] {'chan'}, use_global_device_ids=true, to_apply=%region_1.1 | all-reduce | flops 8192 | bytes 32768 | tf_op jit(solution)/shard_map/while/body/eval_jaxpr/psum | solution.py:13
  785.6 104.5 %psum.39 = bf16[1,1,2,4096]{3,2,1,0:T(2,128)(2,1)S(1)} all-reduce(bf16[1,1,2,4096]{3,2,1,0:T(2,128)(2,1)S(1)} %broadcast_select_fusion.2), channel_id=1, replica_groups=mesh['chan'=32,'day'=8] {'chan'}, use_global_device_ids=true, to_apply=%region_1.1 | all-reduce | flops 8192 | bytes 32768 | tf_op jit(solution)/shard_map/while/body/eval_jaxpr/psum | solution.py:13
  895.3 104.5 %psum.39 = bf16[1,1,2,4096]{3,2,1,0:T(2,128)(2,1)S(1)} all-reduce(bf16[1,1,2,4096]{3,2,1,0:T(2,128)(2,1)S(1)} %broadcast_select_fusion.2), channel_id=1, replica_groups=mesh['chan'=32,'day'=8] {'chan'}, use_global_device_ids=true, to_apply=%region_1.1 | all-reduce | flops 8192 | bytes 32768 | tf_op jit(solution)/shard_map/while/body/eval_jaxpr/psum | solution.py:13
  1005.1 104.5 %psum.39 = bf16[1,1,2,4096]{3,2,1,0:T(2,128)(2,1)S(1)} all-reduce(bf16[1,1,2,4096]{3,2,1,0:T(2,128)(2,1)S(1)} %broadcast_select_fusion.2), channel_id=1, replica_groups=mesh['chan'=32,'day'=8] {'chan'}, use_global_device_ids=true, to_apply=%region_1.1 | all-reduce | flops 8192 | bytes 32768 | tf_op jit(solution)/shard_map/while/body/eval_jaxpr/psum | solution.py:13
  1114.8 104.5 %psum.39 = bf16[1,1,2,4096]{3,2,1,0:T(2,128)(2,1)S(1)} all-reduce(bf16[1,1,2,4096]{3,2,1,0:T(2,128)(2,1)S(1)} %broadcast_select_fusion.2), channel_id=1, replica_groups=mesh['chan'=32,'day'=8] {'chan'}, use_global_device_ids=true, to_apply=%region_1.1 | all-reduce | flops 8192 | bytes 32768 | tf_op jit(solution)/shard_map/while/body/eval_jaxpr/psum | solution.py:13
  1224.5 104.5 %psum.39 = bf16[1,1,2,4096]{3,2,1,0:T(2,128)(2,1)S(1)} all-reduce(bf16[1,1,2,4096]{3,2,1,0:T(2,128)(2,1)S(1)} %broadcast_select_fusion.2), channel_id=1, replica_groups=mesh['chan'=32,'day'=8] {'chan'}, use_global_device_ids=true, to_apply=%region_1.1 | all-reduce | flops 8192 | bytes 32768 | tf_op jit(solution)/shard_map/while/body/eval_jaxpr/psum | solution.py:13
  1334.3 104.5 %psum.39 = bf16[1,1,2,4096]{3,2,1,0:T(2,128)(2,1)S(1)} all-reduce(bf16[1,1,2,4096]{3,2,1,0:T(2,128)(2,1)S(1)} %broadcast_select_fusion.2), channel_id=1, replica_groups=mesh['chan'=32,'day'=8] {'chan'}, use_global_device_ids=true, to_apply=%region_1.1 | all-reduce | flops 8192 | bytes 32768 | tf_op jit(solution)/shard_map/while/body/eval_jaxpr/psum | solution.py:13
  1444.0 104.5 %psum.39 = bf16[1,1,2,4096]{3,2,1,0:T(2,128)(2,1)S(1)} all-reduce(bf16[1,1,2,4096]{3,2,1,0:T(2,128)(2,1)S(1)} %broadcast_select_fusion.2), channel_id=1, replica_groups=mesh['chan'=32,'day'=8] {'chan'}, use_global_device_ids=true, to_apply=%region_1.1 | all-reduce | flops 8192 | bytes 32768 | tf_op jit(solution)/shard_map/while/body/eval_jaxpr/psum | solution.py:13
  1553.7 104.5 %psum.39 = bf16[1,1,2,4096]{3,2,1,0:T(2,128)(2,1)S(1)} all-reduce(bf16[1,1,2,4096]{3,2,1,0:T(2,128)(2,1)S(1)} %broadcast_select_fusion.2), channel_id=1, replica_groups=mesh['chan'=32,'day'=8] {'chan'}, use_global_device_ids=true, to_apply=%region_1.1 | all-reduce | flops 8192 | bytes 32768 | tf_op jit(solution)/shard_map/while/body/eval_jaxpr/psum | solution.py:13
  1663.5 104.5 %psum.39 = bf16[1,1,2,4096]{3,2,1,0:T(2,128)(2,1)S(1)} all-reduce(bf16[1,1,2,4096]{3,2,1,0:T(2,128)(2,1)S(1)} %broadcast_select_fusion.2), channel_id=1, replica_groups=mesh['chan'=32,'day'=8] {'chan'}, use_global_device_ids=true, to_apply=%region_1.1 | all-reduce | flops 8192 | bytes 32768 | tf_op jit(solution)/shard_map/while/body/eval_jaxpr/psum | solution.py:13
  1768.7 17.1 multiply_convert_fusion.1
  1787.6 1.9 fusion.3
  1789.7 85.9 %all-reduce.4.cloned.1.call-done = f32[16,16,256]{2,1,0:T(8,128)} async-done(((f32[16,16,256]{2,1,0:T(8,128)}), f32[16,16,256]{2,1,0:T(8,128)}) %all-reduce.4.cloned.1.call-update) | async-done | bytes 262160 | tf_op jit(solution)/shard_map/psum | solution.py:65
  1875.5 2.1 multiply_reduce_fusion
  1877.8 58.7 %all-reduce.1 = (f32[1,8]{1,0:T(1,128)S(1)}, f32[1,8]{1,0:T(1,128)S(1)}) all-reduce(f32[1,8]{1,0:T(1,128)S(1)} %bitcast.31, f32[1,8]{1,0:T(1,128)S(1)} %bitcast.30), channel_id=1, replica_groups=mesh['chan'=32,'day'=8] {'chan'}, use_global_device_ids=true, to_apply=%region_6.7 | all-reduce | flops 16 | bytes 128 | tf_op jit(solution)/shard_map/psum | solution.py:85
  (66 shorter events, 35.2 us)
Async XLA Ops:
  7.2 1868.4 %all-reduce.4.cloned.1.call-start = ((), (), s32[]{:S(2)}) async-start(), calls=%async_computation | async-start | bytes 524288 | tf_op jit(solution)/shard_map/psum | solution.py:65
  1787.6 2.0 copy-start
  1787.6 90.0 %copy-start.1 = (s32[16]{0:T(128)S(1)}, s32[16]{0:T(128)}, u32[]{:S(2)}) copy-start(s32[16]{0:T(128)} %param.8) | copy-start | bytes 196
Sparse Core Ops, SparseCore 0:
  1789.7 85.8 all-reduce.3
where the time goes:
time: 1950 us; the launch traced here: 1940 us
  blocking collectives  1730 us (89%)
  waiting for transfers between devices  85.9 us (4%)
  loops' own time  52.4 us (3%)
  other arithmetic  34.2 us (2%)
  local copies, waits for them, and re-layouts  22.6 us (1%)
    psum x16, blocking collectives, from_root(): return lax.psum(kept, axis)  1670 us
    psum x1, waiting for transfers between devices, per_device(): total = lax.psum(local_sum, 'day')  85.9 us
    psum x1, blocking collectives, per_device(): lax.psum((jnp.stack(numers, 0), jnp.stack(denoms, 0)), 'chan')  58.7 us
    another operation x1, loops' own time, per_device(): lax.fori_loop(0, nsrc, fetch, jnp.zeros((day_dev, nsrc, 2, bins), jnp.bfl...  52.4 us
  transfers between devices with their start and end apart: 1, of which 1 were waited for; matrix products, arithmetic and copies ran while one was open for 0% of the time, Pallas kernels for 0%

commit v1 on v0

--- a/solution.py
+++ b/solution.py
@@ -8,9 +8,15 @@
 NINT = 8
 
 
+def gather_and_add(x, name):
+    shards = lax.all_gather(x, name, axis=0, tiled=False)
+    total = shards.sum(axis=0)
+    return total
+
+
 def from_root(value, axis, source):
     kept = jnp.where(lax.axis_index(axis) == source, value, 0).astype(value.dtype)
-    return lax.psum(kept, axis)
+    return gather_and_add(kept, axis)
 
 
 def lag_table(bins, lags):

time: 1950 us -> 807 us (0.41)
  blocking collectives: 1730 us -> 591 us
    psum x16 -> x0, blocking collectives: 1670 us -> none  [from_root(): return lax.psum(kept, axis)]
    all_gather x0 -> x16, blocking collectives: none -> 532 us  [gather_and_add(): shards = lax.all_gather(x, name, axis=0, tiled=False)]
where the time goes in v1:
time: 807 us; the launch traced here: 804 us
  blocking collectives  591 us (73%)
  waiting for transfers between devices  80.6 us (10%)
  loops' own time  52.5 us (7%)
  other arithmetic  41.2 us (5%)
  local copies, waits for them, and re-layouts  22.6 us (3%)
  between operations  14.2 us (2%)
    all_gather x16, blocking collectives, gather_and_add(): shards = lax.all_gather(x, name, axis=0, tiled=False)  532 us
    psum x1, waiting for transfers between devices, per_device(): total = lax.psum(local_sum, 'day')  80.6 us
    psum x1, blocking collectives, per_device(): lax.psum((jnp.stack(numers, 0), jnp.stack(denoms, 0)), 'chan')  58.7 us
    another operation x1, loops' own time, per_device(): lax.fori_loop(0, nsrc, fetch, jnp.zeros((day_dev, nsrc, 2, bins), jnp.bfl...  52.5 us
    dynamic_slice x16, local copies, waits for them, and re-layouts, fetch(): chosen_chan = source_index[source]  19.9 us
    another operation x2, other arithmetic  18.2 us
  transfers between devices with their start and end apart: 1, of which 1 were waited for; matrix products, arithmetic and copies ran while one was open for 0% of the time, Pallas kernels for 0%

profile of v1, /device:TPU:1, one launch (start us, length us, event | category | flops | bytes accessed | tf_op | source)
XLA Modules:
  0.0 803.9 jit_solution(11513031456762426176)
XLA Ops:
  9.0 623.7 %while.20 = (s32[]{:T(128)}, bf16[1,16,2,4096]{3,2,1,0:T(2,128)(2,1)S(1)}, s32[16]{0:T(128)}, bf16[1,16,2,4096]{3,2,1,0:T(2,128)(2,1)}, s32[]{:T(128)}, /*index=...) while((s32[]{:T(128)}, ...), condition=%wide.region_2.3_spmd, body=%wide.region_0.2_spmd.sunk | while | flops 262170 | bytes 1147277 | solution.py:46
  9.0 1.2 dynamic_slice.31
  14.2 39.9 %all-gather.2 = bf16[32,1,2,4096]{3,2,1,0:T(2,128)(2,1)S(1)} all-gather(bf16[1,1,2,4096]{3,2,1,0:T(2,128)(2,1)S(1)} %broadcast_select_fusion.2), channel_id=2, replica_groups=mesh['chan'=32,'day'=8] {'chan'}, dimensions={0}, use_global_device_ids=true | all-gather | bytes 540672 | tf_op jit(solution)/shard_map/while/body/eval_jaxpr/all_gather | solution.py:12
  59.8 32.1 %all-gather.2 = bf16[32,1,2,4096]{3,2,1,0:T(2,128)(2,1)S(1)} all-gather(bf16[1,1,2,4096]{3,2,1,0:T(2,128)(2,1)S(1)} %broadcast_select_fusion.2), channel_id=2, replica_groups=mesh['chan'=32,'day'=8] {'chan'}, dimensions={0}, use_global_device_ids=true | all-gather | bytes 540672 | tf_op jit(solution)/shard_map/while/body/eval_jaxpr/all_gather | solution.py:12
  97.7 33.6 %all-gather.2 = bf16[32,1,2,4096]{3,2,1,0:T(2,128)(2,1)S(1)} all-gather(bf16[1,1,2,4096]{3,2,1,0:T(2,128)(2,1)S(1)} %broadcast_select_fusion.2), channel_id=2, replica_groups=mesh['chan'=32,'day'=8] {'chan'}, dimensions={0}, use_global_device_ids=true | all-gather | bytes 540672 | tf_op jit(solution)/shard_map/while/body/eval_jaxpr/all_gather | solution.py:12
  131.8 1.2 dynamic_slice.31
  137.0 32.1 %all-gather.2 = bf16[32,1,2,4096]{3,2,1,0:T(2,128)(2,1)S(1)} all-gather(bf16[1,1,2,4096]{3,2,1,0:T(2,128)(2,1)S(1)} %broadcast_select_fusion.2), channel_id=2, replica_groups=mesh['chan'=32,'day'=8] {'chan'}, dimensions={0}, use_global_device_ids=true | all-gather | bytes 540672 | tf_op jit(solution)/shard_map/while/body/eval_jaxpr/all_gather | solution.py:12
  174.8 33.6 %all-gather.2 = bf16[32,1,2,4096]{3,2,1,0:T(2,128)(2,1)S(1)} all-gather(bf16[1,1,2,4096]{3,2,1,0:T(2,128)(2,1)S(1)} %broadcast_select_fusion.2), channel_id=2, replica_groups=mesh['chan'=32,'day'=8] {'chan'}, dimensions={0}, use_global_device_ids=true | all-gather | bytes 540672 | tf_op jit(solution)/shard_map/while/body/eval_jaxpr/all_gather | solution.py:12
  214.2 32.1 %all-gather.2 = bf16[32,1,2,4096]{3,2,1,0:T(2,128)(2,1)S(1)} all-gather(bf16[1,1,2,4096]{3,2,1,0:T(2,128)(2,1)S(1)} %broadcast_select_fusion.2), channel_id=2, replica_groups=mesh['chan'=32,'day'=8] {'chan'}, dimensions={0}, use_global_device_ids=true | all-gather | bytes 540672 | tf_op jit(solution)/shard_map/while/body/eval_jaxpr/all_gather | solution.py:12
  252.0 33.6 %all-gather.2 = bf16[32,1,2,4096]{3,2,1,0:T(2,128)(2,1)S(1)} all-gather(bf16[1,1,2,4096]{3,2,1,0:T(2,128)(2,1)S(1)} %broadcast_select_fusion.2), channel_id=2, replica_groups=mesh['chan'=32,'day'=8] {'chan'}, dimensions={0}, use_global_device_ids=true | all-gather | bytes 540672 | tf_op jit(solution)/shard_map/while/body/eval_jaxpr/all_gather | solution.py:12
  291.4 32.1 %all-gather.2 = bf16[32,1,2,4096]{3,2,1,0:T(2,128)(2,1)S(1)} all-gather(bf16[1,1,2,4096]{3,2,1,0:T(2,128)(2,1)S(1)} %broadcast_select_fusion.2), channel_id=2, replica_groups=mesh['chan'=32,'day'=8] {'chan'}, dimensions={0}, use_global_device_ids=true | all-gather | bytes 540672 | tf_op jit(solution)/shard_map/while/body/eval_jaxpr/all_gather | solution.py:12
  329.2 33.6 %all-gather.2 = bf16[32,1,2,4096]{3,2,1,0:T(2,128)(2,1)S(1)} all-gather(bf16[1,1,2,4096]{3,2,1,0:T(2,128)(2,1)S(1)} %broadcast_select_fusion.2), channel_id=2, replica_groups=mesh['chan'=32,'day'=8] {'chan'}, dimensions={0}, use_global_device_ids=true | all-gather | bytes 540672 | tf_op jit(solution)/shard_map/while/body/eval_jaxpr/all_gather | solution.py:12
  368.5 32.1 %all-gather.2 = bf16[32,1,2,4096]{3,2,1,0:T(2,128)(2,1)S(1)} all-gather(bf16[1,1,2,4096]{3,2,1,0:T(2,128)(2,1)S(1)} %broadcast_select_fusion.2), channel_id=2, replica_groups=mesh['chan'=32,'day'=8] {'chan'}, dimensions={0}, use_global_device_ids=true | all-gather | bytes 540672 | tf_op jit(solution)/shard_map/while/body/eval_jaxpr/all_gather | solution.py:12
  406.4 33.6 %all-gather.2 = bf16[32,1,2,4096]{3,2,1,0:T(2,128)(2,1)S(1)} all-gather(bf16[1,1,2,4096]{3,2,1,0:T(2,128)(2,1)S(1)} %broadcast_select_fusion.2), channel_id=2, replica_groups=mesh['chan'=32,'day'=8] {'chan'}, dimensions={0}, use_global_device_ids=true | all-gather | bytes 540672 | tf_op jit(solution)/shard_map/while/body/eval_jaxpr/all_gather | solution.py:12
  445.7 32.1 %all-gather.2 = bf16[32,1,2,4096]{3,2,1,0:T(2,128)(2,1)S(1)} all-gather(bf16[1,1,2,4096]{3,2,1,0:T(2,128)(2,1)S(1)} %broadcast_select_fusion.2), channel_id=2, replica_groups=mesh['chan'=32,'day'=8] {'chan'}, dimensions={0}, use_global_device_ids=true | all-gather | bytes 540672 | tf_op jit(solution)/shard_map/while/body/eval_jaxpr/all_gather | solution.py:12
  483.6 33.6 %all-gather.2 = bf16[32,1,2,4096]{3,2,1,0:T(2,128)(2,1)S(1)} all-gather(bf16[1,1,2,4096]{3,2,1,0:T(2,128)(2,1)S(1)} %broadcast_select_fusion.2), channel_id=2, replica_groups=mesh['chan'=32,'day'=8] {'chan'}, dimensions={0}, use_global_device_ids=true | all-gather | bytes 540672 | tf_op jit(solution)/shard_map/while/body/eval_jaxpr/all_gather | solution.py:12
  522.9 32.1 %all-gather.2 = bf16[32,1,2,4096]{3,2,1,0:T(2,128)(2,1)S(1)} all-gather(bf16[1,1,2,4096]{3,2,1,0:T(2,128)(2,1)S(1)} %broadcast_select_fusion.2), channel_id=2, replica_groups=mesh['chan'=32,'day'=8] {'chan'}, dimensions={0}, use_global_device_ids=true | all-gather | bytes 540672 | tf_op jit(solution)/shard_map/while/body/eval_jaxpr/all_gather | solution.py:12
  560.7 33.6 %all-gather.2 = bf16[32,1,2,4096]{3,2,1,0:T(2,128)(2,1)S(1)} all-gather(bf16[1,1,2,4096]{3,2,1,0:T(2,128)(2,1)S(1)} %broadcast_select_fusion.2), channel_id=2, replica_groups=mesh['chan'=32,'day'=8] {'chan'}, dimensions={0}, use_global_device_ids=true | all-gather | bytes 540672 | tf_op jit(solution)/shard_map/while/body/eval_jaxpr/all_gather | solution.py:12
  600.1 32.1 %all-gather.2 = bf16[32,1,2,4096]{3,2,1,0:T(2,128)(2,1)S(1)} all-gather(bf16[1,1,2,4096]{3,2,1,0:T(2,128)(2,1)S(1)} %broadcast_select_fusion.2), channel_id=2, replica_groups=mesh['chan'=32,'day'=8] {'chan'}, dimensions={0}, use_global_device_ids=true | all-gather | bytes 540672 | tf_op jit(solution)/shard_map/while/body/eval_jaxpr/all_gather | solution.py:12
  633.5 17.1 %multiply_convert_fusion.1 = (bf16[4096,256]{1,0:T(8,128)(2,1)S(1)}, bf16[4096,256]{1,0:T(8,128)(2,1)S(1)}) fusion(s32[256]{0:T(256)S(1)} %iota_add_fusion), kind=kLoop, calls=%fused_computation.16 | loop fusion | flops 19922944 | bytes 4195328 | tf_op jit(solution)/shard_map/convert.7
  652.4 1.9 fusion.3
  654.4 80.6 %all-reduce.4.cloned.1.call-done = f32[16,16,256]{2,1,0:T(8,128)} async-done(((f32[16,16,256]{2,1,0:T(8,128)}), f32[16,16,256]{2,1,0:T(8,128)}) %all-reduce.4.cloned.1.call-update) | async-done | bytes 262160 | tf_op jit(solution)/shard_map/psum | solution.py:71
  735.0 2.1 multiply_reduce_fusion
  737.3 58.7 %all-reduce.1 = (f32[1,8]{1,0:T(1,128)S(1)}, f32[1,8]{1,0:T(1,128)S(1)}) all-reduce(f32[1,8]{1,0:T(1,128)S(1)} %bitcast.35, f32[1,8]{1,0:T(1,128)S(1)} %bitcast.34), channel_id=1, replica_groups=mesh['chan'=32,'day'=8] {'chan'}, use_global_device_ids=true, to_apply=%region_6.7 | all-reduce | flops 16 | bytes 128 | tf_op jit(solution)/shard_map/psum | solution.py:91
  (82 shorter events, 42.1 us)
Async XLA Ops:
  7.2 727.9 %all-reduce.4.cloned.1.call-start = ((), (), s32[]{:S(2)}) async-start(), calls=%async_computation | async-start | bytes 524288 | tf_op jit(solution)/shard_map/psum | solution.py:71
  652.3 2.0 copy-start
  652.3 84.8 %copy-start.1 = (s32[16]{0:T(128)S(1)}, s32[16]{0:T(128)}, u32[]{:S(2)}) copy-start(s32[16]{0:T(128)} %param.8) | copy-start | bytes 196
Sparse Core Ops, SparseCore 0:
  654.4 80.5 all-reduce.3
